TPU v7x, 32 devices: a whole 2x2x4 slice. The times are simulated.
32 devices in a mesh: row: 4 (over x, core), col: 8 (over z, y).
Axes of the slice: x: 2, y: 2, z: 4, core: 2. Of those that a mesh axis runs over, the one named last changes fastest.
Arguments:
- tile_list: int32 [512, 2], P(('row', 'col')), may hold values from -1 to 63, as said below
- tile_values: bfloat16 [512, 512, 512], P(('row', 'col'))
- block_order: int32 [64], replicated, may hold values from 0 to 63, as said below
- basis: bfloat16 [64, 512, 256], P(('row', 'col')), may hold values from -8 to 8
Outputs:
- basis_out: bfloat16 [64, 512, 256], P(('row', 'col'))
- projected: float32 [256, 256], replicated
Inputs may be any that keep to these rules, and one draw needn't show every extreme that they name: `block_order`: A permutation of the channel blocks; slot p lies on device p // 2 in row-major order of (row, col). `tile_list`: slots of device (i, j) hold tiles whose row block sits in a slot of a device of row index i and whose column block sits in a slot of a device of column index j; each unordered pair of blocks appears at most once in all; empty slots hold -1 in both columns and may stand anywhere among a device's slots; every device holds at most 16 tiles and some device holds exactly 16.
All inputs are finite; a program needn't handle non-finite values.
Results may differ from a plain program's by a relative error of at most 0.0017.
Values may be sent and summed in bfloat16 or wider, within the bound.
A program may use at most 128 MiB of HBM per device.

v0:
```python
import jax
import jax.numpy as jnp
from jax import lax
from jax.sharding import PartitionSpec as P


def per_device(tile_list, tile_values, block_order, basis):
    rows_count = lax.axis_size("row")
    cols_count = lax.axis_size("col")
    own_blocks = basis.shape[0]
    edge = basis.shape[1]
    rank = basis.shape[2]
    blocks_all = block_order.shape[0]
    scale = jnp.sqrt(jnp.float32(blocks_all * edge))
    row_here = lax.axis_index("row")
    row_group = own_blocks * cols_count
    col_group = own_blocks * rows_count
    present = tile_list[:, 0] >= 0
    slot_range = jnp.arange(blocks_all, dtype=jnp.int32)
    ids_both = jnp.where(present[:, None], tile_list, 0)
    match = block_order[None, None, :] == ids_both[:, :, None]
    slots_both = jnp.sum(jnp.where(match, slot_range[None, None, :], 0), axis=2)
    first_slot = slots_both[:, 0]
    second_slot = slots_both[:, 1]
    row_local = jnp.where(present, first_slot - row_here * row_group, row_group)
    owner_second = second_slot // own_blocks
    col_local = jnp.where(
        present, owner_second // cols_count * own_blocks + second_slot % own_blocks, col_group
    )
    column_side = lax.all_gather(basis, "row", axis=0, tiled=True)
    row_side = lax.all_gather(basis, "col", axis=0, tiled=True)
    empty_block = jnp.zeros((1, edge, rank), basis.dtype)
    column_padded = jnp.concatenate([column_side, empty_block], axis=0)
    row_padded = jnp.concatenate([row_side, empty_block], axis=0)
    picked_col = column_padded[col_local]
    picked_row = row_padded[row_local]
    near_prod = jnp.einsum(
        "tab,tbk->tak", tile_values, picked_col, preferred_element_type=jnp.float32
    )
    far_prod = jnp.einsum(
        "tba,tbk->tak", tile_values, picked_row, preferred_element_type=jnp.float32
    )
    col_partial = (
        jnp.zeros((col_group, edge, rank), jnp.float32).at[col_local].add(far_prod, mode="drop")
    )
    row_partial = (
        jnp.zeros((row_group, edge, rank), jnp.float32).at[row_local].add(near_prod, mode="drop")
    )
    row_owned = lax.psum_scatter(row_partial, "col", scatter_dimension=0, tiled=True)
    upper_part = lax.optimization_barrier(col_partial.astype(jnp.bfloat16))
    remainder = col_partial - upper_part.astype(jnp.float32)
    middle_part = lax.optimization_barrier(remainder.astype(jnp.bfloat16))
    lower_part = (remainder - middle_part.astype(jnp.float32)).astype(jnp.bfloat16)
    pieces = jnp.concatenate([upper_part, middle_part, lower_part], axis=2)
    folded = jnp.einsum("sak,saj->kj", column_side, pieces, preferred_element_type=jnp.float32)
    tile_form = folded[:, :rank] + folded[:, rank : 2 * rank] + folded[:, 2 * rank :]
    projected = lax.psum((tile_form + tile_form.T) / scale, ("row", "col"))
    col_owned = lax.psum_scatter(col_partial, "row", scatter_dimension=0, tiled=True)
    product = (row_owned + col_owned).reshape(own_blocks * edge, rank)
    gram_term = jnp.dot(product.T, product, precision=lax.Precision.HIGHEST)
    gram = lax.psum(gram_term, ("row", "col"))
    first_factor = jnp.linalg.cholesky(gram)
    first_basis = lax.linalg.triangular_solve(
        first_factor, product, left_side=False, lower=True, transpose_a=True
    )
    second_term = jnp.dot(first_basis.T, first_basis, precision=lax.Precision.HIGHEST)
    second = lax.psum(second_term, ("row", "col"))
    second_factor = jnp.linalg.cholesky(second)
    final = lax.linalg.triangular_solve(
        second_factor, first_basis, left_side=False, lower=True, transpose_a=True
    )
    basis_out = (final * scale).astype(jnp.bfloat16).reshape(own_blocks, edge, rank)
    return (basis_out, projected)


def solution(mesh):
    in_specs = (
        P(("row", "col"), None),
        P(("row", "col"), None, None),
        P(),
        P(("row", "col"), None, None),
    )
    out_specs = (P(("row", "col"), None, None), P())
    return jax.shard_map(
        per_device, mesh=mesh, in_specs=in_specs, out_specs=out_specs, check_vma=False
    )
```

profile of v0, /device:TPU:0, one launch (start us, length us, event | category | flops | bytes accessed | tf_op | source)
XLA Modules:
  0.0 729.1 jit_solution(8188007919640402378)
XLA Ops:
  11.6 74.0 %all-gather.5.cloned.1.call-done = bf16[16,512,256]{2,1,0:T(8,128)(2,1)} async-done(((bf16[2,512,256]{2,1,0:T(8,128)(2,1)}), bf16[16,512,256]{2,1,0:T(8,128)(2,1)}) %all-gather.5.cloned.1.call-update) | async-done | bytes 4194320 | tf_op jit(solution)/shard_map/all_gather | solution.py:31
  85.6 4.6 concatenate.13
  90.3 5.2 gather_fusion.1
  95.5 10.3 %convolution_bitcast_fusion = f32[16,512,256]{1,2,0:T(8,128)} fusion(bf16[16,512,256]{2,1,0:T(8,128)(2,1)} %gather_fusion.1, bf16[16,512,512]{2,1,0:T(8,128)(2,1)} %param.8), kind=kOutput, calls=%fused_computation.16 | convolution fusion | flops 2147483648 | bytes 20971520 | tf_op jit(solution)/shard_map/tba,tbk->tak/dot_general | solution.py:40
  105.8 9.3 %copy.39 = f32[16,512,256]{2,1,0:T(8,128)} copy(f32[16,512,256]{1,2,0:T(8,128)} %convolution_bitcast_fusion) | data formatting | bytes 16777216 | tf_op jit(solution)/shard_map/tba,tbk->tak/dot_general | solution.py:40
  115.1 2.3 broadcast_in_dim.54
  117.4 15.6 %scatter_fusion.1 = f32[8,512,256]{2,1,0:T(8,128)} fusion(f32[8,512,256]{2,1,0:T(8,128)} %broadcast_in_dim.54, s32[16]{0:T(128)S(1)} %get-tuple-element.46, f32[16,512,256]{2,1,0:T(8,128)} %copy.39), kind=kCustom, calls=%fused_computation.3 | custom fusion | flops 2097152 | bytes 25165888 | tf_op jit(solution)/shard_map/scatter-add | solution.py:44
  133.1 1.7 concatenate.12
  134.9 2.7 gather_fusion
  137.6 12.1 %convolution_bitcast_fusion.1 = f32[16,512,256]{1,2,0:T(8,128)} fusion(bf16[16,512,256]{2,1,0:T(8,128)(2,1)} %gather_fusion, bf16[16,512,512]{2,1,0:T(8,128)(2,1)} %param.8), kind=kOutput, calls=%fused_computation.17 | convolution fusion | flops 2147483648 | bytes 20971520 | tf_op jit(solution)/shard_map/tab,tbk->tak/dot_general | solution.py:37
  149.7 9.3 %copy.37 = f32[16,512,256]{2,1,0:T(8,128)} copy(f32[16,512,256]{1,2,0:T(8,128)} %convolution_bitcast_fusion.1) | data formatting | bytes 16777216 | tf_op jit(solution)/shard_map/tab,tbk->tak/dot_general | solution.py:37
  159.1 4.1 broadcast_in_dim.47
  163.1 15.9 %scatter_fusion = f32[16,512,256]{2,1,0:T(8,128)} fusion(f32[16,512,256]{2,1,0:T(8,128)} %broadcast_in_dim.47, s32[16]{0:T(128)S(1)} %fusion.37, f32[16,512,256]{2,1,0:T(8,128)} %copy.37), kind=kCustom, calls=%fused_computation.2 | custom fusion | flops 2097152 | bytes 25165888 | tf_op jit(solution)/shard_map/scatter-add | solution.py:47
  179.0 12.8 %all-reduce.7.cloned.1.call-start = ((), (), s32[]{:S(2)}) async-start(), calls=%async_computation.6 | async-start | bytes 524288 | tf_op jit(solution)/shard_map/psum | solution.py:61
  191.9 5.4 copy.46
  197.2 2.6 convert_element_type.19
  203.1 1.8 fusion.7
  205.1 124.2 %reduce-scatter.3.cloned.1.call-done = f32[2,512,256]{2,1,0:T(8,128)} async-done(((f32[16,512,256]{2,1,0:T(8,128)}), f32[2,512,256]{2,1,0:T(8,128)}) %reduce-scatter.3.cloned.1.call-update) | async-done | bytes 1048592 | tf_op jit(solution)/shard_map/reduce_scatter | solution.py:49
  331.0 2.5 convolution_bitcast_fusion.2
  334.3 126.6 %all-reduce.7.cloned.1.call-done = f32[256,256]{0,1:T(8,128)} async-done(((f32[256,256]{0,1:T(8,128)}), f32[256,256]{0,1:T(8,128)}) %all-reduce.7.cloned.1.call-update) | async-done | bytes 262160 | tf_op jit(solution)/shard_map/psum | solution.py:61
  463.1 11.7 %cholesky.130 = f32[128,128]{1,0:T(8,128)S(1)} custom-call(f32[128,128]{1,0:T(8,128)S(1)} %cholesky.194), custom_call_target="Cholesky" | custom-call | tf_op jit(solution)/shard_map/jit(cholesky)/cholesky | solution.py:62
  474.9 9.8 %custom-call.13 = f32[1,128,128]{1,2,0:T(8,128)S(1)} custom-call(f32[1,128,128]{2,1,0:T(8,128)S(1)} %get-tuple-element.59), custom_call_target="InvertDiagBlocksLowerTriangular" | custom-call | tf_op jit(solution)/shard_map/jit(cholesky)/cholesky | solution.py:62
  485.1 11.7 %cholesky.147 = f32[128,128]{1,0:T(8,128)S(1)} custom-call(f32[128,128]{1,0:T(8,128)S(1)} %convolution_subtract_fusion.3), custom_call_target="Cholesky" | custom-call | tf_op jit(solution)/shard_map/jit(cholesky)/cholesky | solution.py:62
  499.1 4.1 while.4
  503.2 20.0 %custom-call.14 = f32[2,128,128]{1,2,0:T(8,128)S(1)} custom-call(f32[2,128,128]{2,1,0:T(8,128)S(1)} %get-tuple-element.18), custom_call_target="InvertDiagBlocksLowerTriangular" | custom-call | tf_op jit(solution)/shard_map/triangular_solve/custom-call.0 | solution.py:63
  525.5 1.7 fusion.10
  527.2 128.6 %all-reduce.9.cloned.1.call-done = (f32[256,256]{0,1:T(8,128)}, f32[256,256]{0,1:T(8,128)}) async-done(((f32[256,256]{0,1:T(8,128)}, f32[256,256]{0,1:T(8,128)}), (f32[256,256]{0,1:T(8,128)}, f32[256,256]{0,1:T(8,128)})) %all-reduce.9.cloned.1.call-update) | async-done | bytes 524304 | tf_op jit(solution)/shard_map/psum | solution.py:67
  657.9 11.7 %cholesky.164 = f32[128,128]{1,0:T(8,128)S(1)} custom-call(f32[128,128]{1,0:T(8,128)S(1)} %cholesky.197), custom_call_target="Cholesky" | custom-call | tf_op jit(solution)/shard_map/jit(cholesky)/cholesky | solution.py:68
  669.6 9.8 %custom-call.15 = f32[1,128,128]{1,2,0:T(8,128)S(1)} custom-call(f32[1,128,128]{2,1,0:T(8,128)S(1)} %get-tuple-element.55), custom_call_target="InvertDiagBlocksLowerTriangular" | custom-call | tf_op jit(solution)/shard_map/jit(cholesky)/cholesky | solution.py:68
  679.9 11.9 %cholesky.181 = f32[128,128]{1,0:T(8,128)S(1)} custom-call(f32[128,128]{1,0:T(8,128)S(1)} %convolution_subtract_fusion.2), custom_call_target="Cholesky" | custom-call | tf_op jit(solution)/shard_map/jit(cholesky)/cholesky | solution.py:68
  694.5 4.0 while.5
  698.5 19.7 %custom-call.16 = f32[2,128,128]{1,2,0:T(8,128)S(1)} custom-call(f32[2,128,128]{2,1,0:T(8,128)S(1)} %get-tuple-element.19), custom_call_target="InvertDiagBlocksLowerTriangular" | custom-call | tf_op jit(solution)/shard_map/triangular_solve/custom-call.0 | solution.py:69
  (79 shorter events, 31.9 us)
Async XLA Ops:
  7.2 78.5 %all-gather.5.cloned.1.call-start = ((), (), s32[]{:S(2)}) async-start(), calls=%async_computation.4 | async-start | bytes 4718592 | tf_op jit(solution)/shard_map/all_gather | solution.py:31
  7.9 125.2 %all-gather.3.cloned.1.call-start = ((), (), s32[]{:S(2)}) async-start(), calls=%async_computation.2 | async-start | bytes 2621440 | tf_op jit(solution)/shard_map/all_gather | solution.py:30
  8.6 196.5 %reduce-scatter.5.cloned.1.call-start = ((), (), s32[]{:S(2)}) async-start(), calls=%async_computation.5 | async-start | bytes 5242880 | tf_op jit(solution)/shard_map/reduce_scatter | solution.py:58
  133.0 196.3 %reduce-scatter.3.cloned.1.call-start = ((), (), s32[]{:S(2)}) async-start(), calls=%async_computation.3 | async-start | bytes 9437184 | tf_op jit(solution)/shard_map/reduce_scatter | solution.py:49
  179.0 282.0 %all-reduce.7.cloned.1.call-start = ((), (), s32[]{:S(2)}) async-start(), calls=%async_computation.6 | async-start | bytes 524288 | tf_op jit(solution)/shard_map/psum | solution.py:61
  197.2 3.5 copy-start
  201.5 1.6 copy-start.1
  333.5 322.3 %all-reduce.9.cloned.1.call-start = ((), (), s32[]{:S(2)}) async-start(), calls=%async_computation.7 | async-start | bytes 1048576 | tf_op jit(solution)/shard_map/psum | solution.py:67
  679.7 41.5 %copy-start.2 = (f32[256,256]{0,1:T(8,128)S(1)}, f32[256,256]{0,1:T(8,128)}, u32[]{:S(2)}) copy-start(f32[256,256]{0,1:T(8,128)} %get-tuple-element.43) | copy-start | bytes 786436
Sparse Core Ops, SparseCore 0:
  10.1 75.5 all-gather.4
  87.2 21.0 all-gather.2
  133.1 45.1 reduce-scatter.4
  181.8 147.4 reduce-scatter.2
  335.2 125.7 all-reduce.6
  527.3 128.3 all-reduce.8
where the time goes:
time: 737 us; the launch traced here: 729 us
  waiting for transfers between devices  455 us (62%)
  other arithmetic  152 us (21%)
  local copies, waits for them, and re-layouts  58.5 us (8%)
  matrix products  33.5 us (5%)
  between operations  17.3 us (2%)
  starting transfers between devices  13 us (2%)
    psum x1, waiting for transfers between devices, per_device(): second = lax.psum(second_term, ('row', 'col'))  129 us
    psum x1, waiting for transfers between devices, per_device(): gram = lax.psum(gram_term, ('row', 'col'))  127 us
    reduce_scatter x1, waiting for transfers between devices, per_device(): lax.psum_scatter(row_partial, 'col', scatter_dimension=0, tiled=True)  124 us
    all_gather x1, waiting for transfers between devices, per_device(): row_side = lax.all_gather(basis, 'col', axis=0, tiled=True)  74 us
    another operation x7, other arithmetic, per_device(): second_factor = jnp.linalg.cholesky(second)  34.8 us
    another operation x6, other arithmetic, per_device(): first_factor = jnp.linalg.cholesky(gram)  34 us
    another operation x3, other arithmetic, per_device(): lax.linalg.triangular_solve(first_factor, product, left_side=False, lower...  20 us
    another operation x2, other arithmetic, per_device(): lax.linalg.triangular_solve(second_factor, first_basis, left_side=False,...  19.7 us
  transfers between devices with their start and end apart: 6, of which 4 were waited for; matrix products, arithmetic and copies ran while one was open for 15% of the time, Pallas kernels for 0%

commit v1 on v0

--- a/solution.py
+++ b/solution.py
@@ -2,6 +2,24 @@
 import jax.numpy as jnp
 from jax import lax
 from jax.sharding import PartitionSpec as P
+
+
+def _build_bands(my_data, along_dim):
+    z2 = list(my_data.shape[1:])
+    z2[along_dim] *= my_data.shape[0]
+    return jnp.moveaxis(my_data, 0, along_dim).reshape(z2)
+
+
+def connect_lots_all(obj, along_axis, array_axis):
+    sides = jax.lax.axis_size(along_axis)
+    row_list = [(kk, (kk + 1) % sides) for kk in range(sides)]
+    chunks = [obj]
+    while len(chunks) < sides:
+        aux = jax.lax.ppermute(chunks[-1], along_axis, row_list)
+        chunks.append(aux)
+    known = jax.lax.axis_index(along_axis)
+    chunks = jnp.stack(chunks)[(known - jnp.arange(sides)) % sides]
+    return _build_bands(chunks, array_axis)
 
 
 def per_device(tile_list, tile_values, block_order, basis):
@@ -28,7 +46,7 @@
         present, owner_second // cols_count * own_blocks + second_slot % own_blocks, col_group
     )
     column_side = lax.all_gather(basis, "row", axis=0, tiled=True)
-    row_side = lax.all_gather(basis, "col", axis=0, tiled=True)
+    row_side = connect_lots_all(basis, "col", 0)
     empty_block = jnp.zeros((1, edge, rank), basis.dtype)
     column_padded = jnp.concatenate([column_side, empty_block], axis=0)
     row_padded = jnp.concatenate([row_side, empty_block], axis=0)

time: 737 us -> 762 us (1.034)
  local copies, waits for them, and re-layouts: 58.5 us -> 71.2 us
  waiting for transfers between devices: 455 us -> 464 us
    ppermute x0 -> x7, waiting for transfers between devices: none -> 87.5 us  [connect_lots_all(): aux = jax.lax.ppermute(chunks[-1], along_axis, row_list)]
    all_gather x1 -> x0, waiting for transfers between devices: 74 us -> none  [per_device(): row_side = lax.all_gather(basis, 'col', axis=0, tiled=True)]
  transfers between devices with their start and end apart: 6 -> 12, of which waited for: 4 -> 10; matrix products, arithmetic and copies ran while one was open for 15% -> 16% of each run, Pallas kernels for 0% -> 0%
where the time goes in v1:
time: 762 us; the launch traced here: 754 us
  waiting for transfers between devices  464 us (61%)
  other arithmetic  152 us (20%)
  local copies, waits for them, and re-layouts  71.2 us (9%)
  matrix products  33 us (4%)
  between operations  17 us (2%)
  starting transfers between devices  16 us (2%)
    psum x1, waiting for transfers between devices, per_device(): second = lax.psum(second_term, ('row', 'col'))  129 us
    psum x1, waiting for transfers between devices, per_device(): gram = lax.psum(gram_term, ('row', 'col'))  127 us
    reduce_scatter x1, waiting for transfers between devices, per_device(): lax.psum_scatter(row_partial, 'col', scatter_dimension=0, tiled=True)  122 us
    ppermute x7, waiting for transfers between devices, connect_lots_all(): aux = jax.lax.ppermute(chunks[-1], along_axis, row_list)  87.5 us
    another operation x7, other arithmetic, per_device(): second_factor = jnp.linalg.cholesky(second)  34.8 us
    another operation x6, other arithmetic, per_device(): first_factor = jnp.linalg.cholesky(gram)  34 us
    another operation x3, other arithmetic, per_device(): lax.linalg.triangular_solve(first_factor, product, left_side=False, lower...  20 us
    another operation x2, other arithmetic, per_device(): lax.linalg.triangular_solve(second_factor, first_basis, left_side=False,...  19.7 us
  transfers between devices with their start and end apart: 12, of which 10 were waited for; matrix products, arithmetic and copies ran while one was open for 16% of the time, Pallas kernels for 0%

profile of v1, /device:TPU:0, one launch (start us, length us, event | category | flops | bytes accessed | tf_op | source)
XLA Modules:
  0.0 753.6 jit_solution(15524739183040842581)
XLA Ops:
  10.3 15.2 %collective-permute-done = bf16[2,512,256]{2,1,0:T(8,128)(2,1)S(1)} collective-permute-done((bf16[2,512,256]{2,1,0:T(8,128)(2,1)}, bf16[2,512,256]{2,1,0:T(8,128)(2,1)S(1)}, u32[]{:S(2)}, u32[]{:S(2)}) %collective-permute-start) | collective-permute-done | bytes 524320 | tf_op jit(solution)/shard_map/ppermute | solution.py:18
  25.4 15.8 %collective-permute-done.1 = bf16[2,512,256]{2,1,0:T(8,128)(2,1)S(1)} collective-permute-done((bf16[2,512,256]{2,1,0:T(8,128)(2,1)S(1)}, bf16[2,512,256]{2,1,0:T(8,128)(2,1)S(1)}, u32[]{:S(2)}, u32[]{:S(2)}) %collective-permute-start.1) | collective-permute-done | bytes 524320 | tf_op jit(solution)/shard_map/ppermute | solution.py:18
  42.0 14.2 %collective-permute-done.2 = bf16[2,512,256]{2,1,0:T(8,128)(2,1)S(1)} collective-permute-done((bf16[2,512,256]{2,1,0:T(8,128)(2,1)S(1)}, bf16[2,512,256]{2,1,0:T(8,128)(2,1)S(1)}, u32[]{:S(2)}, u32[]{:S(2)}) %collective-permute-start.2) | collective-permute-done | bytes 524320 | tf_op jit(solution)/shard_map/ppermute | solution.py:18
  58.4 11.8 %collective-permute-done.3 = bf16[2,512,256]{2,1,0:T(8,128)(2,1)S(1)} collective-permute-done((bf16[2,512,256]{2,1,0:T(8,128)(2,1)S(1)}, bf16[2,512,256]{2,1,0:T(8,128)(2,1)S(1)}, u32[]{:S(2)}, u32[]{:S(2)}) %collective-permute-start.3) | collective-permute-done | bytes 524320 | tf_op jit(solution)/shard_map/ppermute | solution.py:18
  72.1 11.3 %collective-permute-done.4 = bf16[2,512,256]{2,1,0:T(8,128)(2,1)S(1)} collective-permute-done((bf16[2,512,256]{2,1,0:T(8,128)(2,1)S(1)}, bf16[2,512,256]{2,1,0:T(8,128)(2,1)S(1)}, u32[]{:S(2)}, u32[]{:S(2)}) %collective-permute-start.4) | collective-permute-done | bytes 524320 | tf_op jit(solution)/shard_map/ppermute | solution.py:18
  86.0 9.8 %collective-permute-done.5 = bf16[2,512,256]{2,1,0:T(8,128)(2,1)S(1)} collective-permute-done((bf16[2,512,256]{2,1,0:T(8,128)(2,1)S(1)}, bf16[2,512,256]{2,1,0:T(8,128)(2,1)S(1)}, u32[]{:S(2)}, u32[]{:S(2)}) %collective-permute-start.5) | collective-permute-done | bytes 524320 | tf_op jit(solution)/shard_map/ppermute | solution.py:18
  98.3 9.4 %collective-permute-done.6 = bf16[2,512,256]{2,1,0:T(8,128)(2,1)S(1)} collective-permute-done((bf16[2,512,256]{2,1,0:T(8,128)(2,1)S(1)}, bf16[2,512,256]{2,1,0:T(8,128)(2,1)S(1)}, u32[]{:S(2)}, u32[]{:S(2)}) %collective-permute-start.6) | collective-permute-done | bytes 524320 | tf_op jit(solution)/shard_map/ppermute | solution.py:18
  108.5 5.0 gather_fusion.1
  113.5 4.6 concatenate.13
  118.1 5.0 gather_fusion.2
  123.1 10.2 %convolution_bitcast_fusion = f32[16,512,256]{1,2,0:T(8,128)} fusion(bf16[16,512,256]{2,1,0:T(8,128)(2,1)} %gather_fusion.2, bf16[16,512,512]{2,1,0:T(8,128)(2,1)} %param.8), kind=kOutput, calls=%fused_computation.17 | convolution fusion | flops 2147483648 | bytes 20971520 | tf_op jit(solution)/shard_map/tba,tbk->tak/dot_general | solution.py:58
  133.4 9.3 %copy.54 = f32[16,512,256]{2,1,0:T(8,128)} copy(f32[16,512,256]{1,2,0:T(8,128)} %convolution_bitcast_fusion) | data formatting | bytes 16777216 | tf_op jit(solution)/shard_map/tba,tbk->tak/dot_general | solution.py:58
  144.9 15.6 %scatter_fusion.1 = f32[8,512,256]{2,1,0:T(8,128)} fusion(f32[8,512,256]{2,1,0:T(8,128)} %broadcast_in_dim.55, s32[16]{0:T(128)S(1)} %get-tuple-element.48, f32[16,512,256]{2,1,0:T(8,128)} %copy.54), kind=kCustom, calls=%fused_computation.4 | custom fusion | flops 2097152 | bytes 25165888 | tf_op jit(solution)/shard_map/scatter-add | solution.py:62
  165.2 11.7 %convolution_bitcast_fusion.1 = f32[16,512,256]{1,2,0:T(8,128)} fusion(bf16[16,512,256]{2,1,0:T(8,128)(2,1)} %gather_fusion, bf16[16,512,512]{2,1,0:T(8,128)(2,1)} %param.8), kind=kOutput, calls=%fused_computation.18 | convolution fusion | flops 2147483648 | bytes 20971520 | tf_op jit(solution)/shard_map/tab,tbk->tak/dot_general | solution.py:55
  176.9 9.5 %copy.52 = f32[16,512,256]{2,1,0:T(8,128)} copy(f32[16,512,256]{1,2,0:T(8,128)} %convolution_bitcast_fusion.1) | data formatting | bytes 16777216 | tf_op jit(solution)/shard_map/tab,tbk->tak/dot_general | solution.py:55
  186.4 4.1 broadcast_in_dim.48
  190.5 16.0 %scatter_fusion = f32[16,512,256]{2,1,0:T(8,128)} fusion(f32[16,512,256]{2,1,0:T(8,128)} %broadcast_in_dim.48, s32[16]{0:T(128)S(1)} %fusion.39, f32[16,512,256]{2,1,0:T(8,128)} %copy.52), kind=kCustom, calls=%fused_computation.3 | custom fusion | flops 2097152 | bytes 25165888 | tf_op jit(solution)/shard_map/scatter-add | solution.py:65
  206.5 12.8 %all-reduce.7.cloned.1.call-start = ((), (), s32[]{:S(2)}) async-start(), calls=%async_computation.5 | async-start | bytes 524288 | tf_op jit(solution)/shard_map/psum | solution.py:79
  219.3 5.4 copy.61
  232.6 121.6 %reduce-scatter.3.cloned.1.call-done = f32[2,512,256]{2,1,0:T(8,128)} async-done(((f32[16,512,256]{2,1,0:T(8,128)}), f32[2,512,256]{2,1,0:T(8,128)}) %reduce-scatter.3.cloned.1.call-update) | async-done | bytes 1048592 | tf_op jit(solution)/shard_map/reduce_scatter | solution.py:67
  359.2 126.7 %all-reduce.7.cloned.1.call-done = f32[256,256]{0,1:T(8,128)} async-done(((f32[256,256]{0,1:T(8,128)}), f32[256,256]{0,1:T(8,128)}) %all-reduce.7.cloned.1.call-update) | async-done | bytes 262160 | tf_op jit(solution)/shard_map/psum | solution.py:79
  487.9 11.7 %cholesky.130 = f32[128,128]{1,0:T(8,128)S(1)} custom-call(f32[128,128]{1,0:T(8,128)S(1)} %cholesky.194), custom_call_target="Cholesky" | custom-call | tf_op jit(solution)/shard_map/jit(cholesky)/cholesky | solution.py:80
  499.7 9.8 %custom-call.13 = f32[1,128,128]{1,2,0:T(8,128)S(1)} custom-call(f32[1,128,128]{2,1,0:T(8,128)S(1)} %get-tuple-element.61), custom_call_target="InvertDiagBlocksLowerTriangular" | custom-call | tf_op jit(solution)/shard_map/jit(cholesky)/cholesky | solution.py:80
  510.0 11.7 %cholesky.147 = f32[128,128]{1,0:T(8,128)S(1)} custom-call(f32[128,128]{1,0:T(8,128)S(1)} %convolution_subtract_fusion.3), custom_call_target="Cholesky" | custom-call | tf_op jit(solution)/shard_map/jit(cholesky)/cholesky | solution.py:80
  524.0 4.1 while.4
  528.1 20.0 %custom-call.14 = f32[2,128,128]{1,2,0:T(8,128)S(1)} custom-call(f32[2,128,128]{2,1,0:T(8,128)S(1)} %get-tuple-element.18), custom_call_target="InvertDiagBlocksLowerTriangular" | custom-call | tf_op jit(solution)/shard_map/triangular_solve/custom-call.0 | solution.py:81
  552.1 128.5 %all-reduce.9.cloned.1.call-done = (f32[256,256]{0,1:T(8,128)}, f32[256,256]{0,1:T(8,128)}) async-done(((f32[256,256]{0,1:T(8,128)}, f32[256,256]{0,1:T(8,128)}), (f32[256,256]{0,1:T(8,128)}, f32[256,256]{0,1:T(8,128)})) %all-reduce.9.cloned.1.call-update) | async-done | bytes 524304 | tf_op jit(solution)/shard_map/psum | solution.py:85
  682.7 11.7 %cholesky.164 = f32[128,128]{1,0:T(8,128)S(1)} custom-call(f32[128,128]{1,0:T(8,128)S(1)} %cholesky.197), custom_call_target="Cholesky" | custom-call | tf_op jit(solution)/shard_map/jit(cholesky)/cholesky | solution.py:86
  694.5 9.8 %custom-call.15 = f32[1,128,128]{1,2,0:T(8,128)S(1)} custom-call(f32[1,128,128]{2,1,0:T(8,128)S(1)} %get-tuple-element.57), custom_call_target="InvertDiagBlocksLowerTriangular" | custom-call | tf_op jit(solution)/shard_map/jit(cholesky)/cholesky | solution.py:86
  704.8 11.9 %cholesky.181 = f32[128,128]{1,0:T(8,128)S(1)} custom-call(f32[128,128]{1,0:T(8,128)S(1)} %convolution_subtract_fusion.2), custom_call_target="Cholesky" | custom-call | tf_op jit(solution)/shard_map/jit(cholesky)/cholesky | solution.py:86
  719.4 4.0 while.5
  723.4 19.7 %custom-call.16 = f32[2,128,128]{1,2,0:T(8,128)S(1)} custom-call(f32[2,128,128]{2,1,0:T(8,128)S(1)} %get-tuple-element.19), custom_call_target="InvertDiagBlocksLowerTriangular" | custom-call | tf_op jit(solution)/shard_map/triangular_solve/custom-call.0 | solution.py:87
  (101 shorter events, 56.8 us)
Async XLA Ops:
  7.2 153.5 %all-gather.2.cloned.1.call-start = ((), (), s32[]{:S(2)}) async-start(), calls=%async_computation.2 | async-start | bytes 2621440 | tf_op jit(solution)/shard_map/all_gather | solution.py:48
  7.2 18.2 %collective-permute-start = (bf16[2,512,256]{2,1,0:T(8,128)(2,1)}, bf16[2,512,256]{2,1,0:T(8,128)(2,1)S(1)}, u32[]{:S(2)}, u32[]{:S(2)}) collective-permute-start(bf16[2,512,256]{2,1,0:T(8,128)(2,1)} %param.10), channel_id=1, source_target_pairs={{0,1},{1,2},{2,3},{3,4},{4,5},{5,6},{6,7},{7,0},{8,9},{9,10},{10,1... | collective-permute-start | bytes 1572872 | tf_op jit(solution)/shard_map/ppermute | solution.py:18
  25.4 15.8 %collective-permute-start.1 = (bf16[2,512,256]{2,1,0:T(8,128)(2,1)S(1)}, bf16[2,512,256]{2,1,0:T(8,128)(2,1)S(1)}, u32[]{:S(2)}, u32[]{:S(2)}) collective-permute-start(bf16[2,512,256]{2,1,0:T(8,128)(2,1)S(1)} %collective-permute-done), channel_id=1, source_target_pairs={{0,1},{1,2},{2,3},{3,4},{4,5},{5,6},{6,7},{7,0},{8,9},{9,10},{10,1... | collective-permute-start | bytes 1572872 | tf_op jit(solution)/shard_map/ppermute | solution.py:18
  41.2 14.9 %collective-permute-start.2 = (bf16[2,512,256]{2,1,0:T(8,128)(2,1)S(1)}, bf16[2,512,256]{2,1,0:T(8,128)(2,1)S(1)}, u32[]{:S(2)}, u32[]{:S(2)}) collective-permute-start(bf16[2,512,256]{2,1,0:T(8,128)(2,1)S(1)} %collective-permute-done.1), channel_id=1, source_target_pairs={{0,1},{1,2},{2,3},{3,4},{4,5},{5,6},{6,7},{7,0},{8,9},{9,10},{10,1... | collective-permute-start | bytes 1572872 | tf_op jit(solution)/shard_map/ppermute | solution.py:18
  41.2 191.3 %reduce-scatter.5.cloned.1.call-start = ((), (), s32[]{:S(2)}) async-start(), calls=%async_computation.4 | async-start | bytes 5242880 | tf_op jit(solution)/shard_map/reduce_scatter | solution.py:76
  56.1 14.1 %collective-permute-start.3 = (bf16[2,512,256]{2,1,0:T(8,128)(2,1)S(1)}, bf16[2,512,256]{2,1,0:T(8,128)(2,1)S(1)}, u32[]{:S(2)}, u32[]{:S(2)}) collective-permute-start(bf16[2,512,256]{2,1,0:T(8,128)(2,1)S(1)} %collective-permute-done.2), channel_id=1, source_target_pairs={{0,1},{1,2},{2,3},{3,4},{4,5},{5,6},{6,7},{7,0},{8,9},{9,10},{10,1... | collective-permute-start | bytes 1572872 | tf_op jit(solution)/shard_map/ppermute | solution.py:18
  70.2 13.2 %collective-permute-start.4 = (bf16[2,512,256]{2,1,0:T(8,128)(2,1)S(1)}, bf16[2,512,256]{2,1,0:T(8,128)(2,1)S(1)}, u32[]{:S(2)}, u32[]{:S(2)}) collective-permute-start(bf16[2,512,256]{2,1,0:T(8,128)(2,1)S(1)} %collective-permute-done.3), channel_id=1, source_target_pairs={{0,1},{1,2},{2,3},{3,4},{4,5},{5,6},{6,7},{7,0},{8,9},{9,10},{10,1... | collective-permute-start | bytes 1572872 | tf_op jit(solution)/shard_map/ppermute | solution.py:18
  83.4 12.4 %collective-permute-start.5 = (bf16[2,512,256]{2,1,0:T(8,128)(2,1)S(1)}, bf16[2,512,256]{2,1,0:T(8,128)(2,1)S(1)}, u32[]{:S(2)}, u32[]{:S(2)}) collective-permute-start(bf16[2,512,256]{2,1,0:T(8,128)(2,1)S(1)} %collective-permute-done.4), channel_id=1, source_target_pairs={{0,1},{1,2},{2,3},{3,4},{4,5},{5,6},{6,7},{7,0},{8,9},{9,10},{10,1... | collective-permute-start | bytes 1572872 | tf_op jit(solution)/shard_map/ppermute | solution.py:18
  95.8 11.9 %collective-permute-start.6 = (bf16[2,512,256]{2,1,0:T(8,128)(2,1)S(1)}, bf16[2,512,256]{2,1,0:T(8,128)(2,1)S(1)}, u32[]{:S(2)}, u32[]{:S(2)}) collective-permute-start(bf16[2,512,256]{2,1,0:T(8,128)(2,1)S(1)} %collective-permute-done.5), channel_id=1, source_target_pairs={{0,1},{1,2},{2,3},{3,4},{4,5},{5,6},{6,7},{7,0},{8,9},{9,10},{10,1... | collective-permute-start | bytes 1572872 | tf_op jit(solution)/shard_map/ppermute | solution.py:18
  160.6 193.6 %reduce-scatter.3.cloned.1.call-start = ((), (), s32[]{:S(2)}) async-start(), calls=%async_computation.3 | async-start | bytes 9437184 | tf_op jit(solution)/shard_map/reduce_scatter | solution.py:67
  206.5 279.3 %all-reduce.7.cloned.1.call-start = ((), (), s32[]{:S(2)}) async-start(), calls=%async_computation.5 | async-start | bytes 524288 | tf_op jit(solution)/shard_map/psum | solution.py:79
  224.7 3.5 copy-start
  229.0 1.6 copy-start.1
  358.4 322.3 %all-reduce.9.cloned.1.call-start = ((), (), s32[]{:S(2)}) async-start(), calls=%async_computation.6 | async-start | bytes 1048576 | tf_op jit(solution)/shard_map/psum | solution.py:85
  704.5 41.5 %copy-start.2 = (f32[256,256]{0,1:T(8,128)S(1)}, f32[256,256]{0,1:T(8,128)}, u32[]{:S(2)}) copy-start(f32[256,256]{0,1:T(8,128)} %get-tuple-element.45) | copy-start | bytes 786436
Sparse Core Ops, SparseCore 0:
  41.4 23.7 all-gather.1
  160.7 42.2 reduce-scatter.4
  206.6 147.4 reduce-scatter.2
  360.1 125.7 all-reduce.6
  552.2 128.3 all-reduce.8
